TPU v7x, 32 devices: a whole 2x2x4 slice. The times are simulated.
32 devices in a mesh: tm: 8 (over y, x, core), group: 4 (over z).
Axes of the slice: x: 2, y: 2, z: 4, core: 2. Of those that a mesh axis runs over, the one named last changes fastest.
Arguments:
- propagators: float32 [8, 384, 384], P('tm'), may hold values from -1 to 1, as said below
- perturbation: float32 [8, 384, 384], P('tm', 'group'), as said below
Outputs:
- gradient: float32 [384, 384], P('tm')
Inputs may be any that keep to these rules, and one draw needn't show every extreme that they name: `propagators`: each slice's matrix is orthogonal. `perturbation`: each slice's matrix is symmetric.
All inputs are finite; a program needn't handle non-finite values.
Results may differ from a plain program's by a relative error of at most 0.00028.
Values sent between devices are 32-bit elements; how exact they have to be, the bound alone decides.
No kernel may reach another device: no remote copies, remote signals or barrier semaphores. Data moves between devices by JAX's collectives and lax.ppermute only.
A program may use at most 128 MiB of HBM per device.

v0:
```python
import jax
import jax.numpy as jnp
from jax import lax
from jax.sharding import PartitionSpec as P


def carried_in(part, axis, combine, identity):
    place = lax.axis_index(axis)
    gathered = lax.all_gather(part, axis)
    state = jnp.zeros_like(part) + jnp.asarray(identity, part.dtype)

    def one(lap, state):
        return combine(state, lax.dynamic_index_in_dim(gathered, lap, 0, False))

    return lax.fori_loop(0, place, one, state)


def times_high(left, right):
    return jnp.dot(left, right, precision=lax.Precision.HIGHEST, preferred_element_type=jnp.float32)


def compose(earlier, later):
    return times_high(later, earlier)


def body(propagators, perturbation):
    slice_count = propagators.shape[0]
    order_dim = propagators.shape[1]
    block_rows = perturbation.shape[1]
    identity = jnp.eye(order_dim, dtype=jnp.float32)
    local_prefixes = [identity]
    device_total = times_high(propagators[slice_count - 1], local_prefixes[-1])
    before = carried_in(device_total, "tm", compose, identity)
    first_block = lax.axis_index("group") * block_rows
    prefix_rows = lax.dynamic_slice_in_dim(before, first_block, block_rows, 0)
    pulled = times_high(perturbation[0], before)
    conjugated = times_high(prefix_rows.T, pulled)
    row_sums = lax.psum_scatter(conjugated, "tm", scatter_dimension=0, tiled=True)
    return lax.psum(row_sums, "group")


def solution(mesh):
    in_specs = (P("tm", None, None), P("tm", "group", None))
    out_specs = P("tm", None)
    return jax.shard_map(body, mesh=mesh, in_specs=in_specs, out_specs=out_specs, check_vma=False)
```

profile of v0, /device:TPU:0, one launch (start us, length us, event | category | flops | bytes accessed | tf_op | source)
XLA Modules:
  0.0 155.6 jit_solution(5823865246684013293)
XLA Ops:
  6.5 0.0 copy-start
  6.5 0.0 all-gather.3.cloned.1.call-start
  6.5 1.1 copy-done
  7.6 1.6 %convolution_bitcast_fusion = f32[384,384]{0,1:T(8,128)} fusion(f32[1,384,384]{2,1,0:T(8,128)S(1)} %copy-done), kind=kOutput, calls=%fused_computation.4 | convolution fusion | flops 679772160 | bytes 1179648 | tf_op jit(solution)/shard_map/dot_general | solution.py:19
  9.2 0.0 all-gather.3.cloned.1.call-update
  9.2 0.0 reduce-scatter.2.cloned.1.call-start
  9.3 41.5 %all-gather.3.cloned.1.call-done = f32[3072,384]{0,1:T(8,128)} async-done(((f32[384,384]{0,1:T(8,128)}), f32[3072,384]{0,1:T(8,128)}) %all-gather.3.cloned.1.call-update) | async-done | bytes 4718608 | tf_op jit(solution)/shard_map/all_gather | solution.py:9
  50.8 6.1 %copy.4 = f32[3072,384]{1,0:T(8,128)} copy(f32[3072,384]{0,1:T(8,128)} %all-gather.3.cloned.1.call-done) | data formatting | bytes 9437184 | tf_op jit(solution)/shard_map/while | solution.py:15
  56.9 0.0 copy-start.1
  56.9 0.9 copy-done.1
  57.8 1.1 fusion.8
  58.9 1.7 %fusion.10 = f32[384,384]{1,0:T(8,128)} fusion(f32[384,96]{1,0:T(8,128)S(1)} %fusion.8, f32[384,384]{1,0:T(8,128)S(1)} %get-tuple-element.28, s32[]{:T(128)S(6)} %select_n.7), kind=kOutput, calls=%fused_computation.11 | convolution fusion | flops 169869312 | bytes 933892 | tf_op jit(solution)/shard_map/dot_general | solution.py:19
  60.6 0.0 reduce-scatter.2.cloned.1.call-update
  60.6 0.0 all-reduce.2.cloned.1.call-start
  60.7 50.3 %reduce-scatter.2.cloned.1.call-done = f32[48,384]{1,0:T(8,128)} async-done(((f32[384,384]{1,0:T(8,128)}), f32[48,384]{1,0:T(8,128)}) %reduce-scatter.2.cloned.1.call-update) | async-done | bytes 73744 | tf_op jit(solution)/shard_map/reduce_scatter | solution.py:38
  111.0 0.0 all-reduce.2.cloned.1.call-update
  111.0 36.6 %all-reduce.2.cloned.1.call-done = f32[48,384]{1,0:T(8,128)} async-done(((f32[48,384]{1,0:T(8,128)}), f32[48,384]{1,0:T(8,128)}) %all-reduce.2.cloned.1.call-update) | async-done | bytes 73744 | tf_op jit(solution)/shard_map/psum | solution.py:39
  147.6 1.5 copy.14
  (2 shorter events, 0.0 us)
Async XLA Ops:
  6.5 1.1 copy-start
  6.5 44.3 %all-gather.3.cloned.1.call-start = ((), (), s32[]{:S(2)}) async-start(), calls=%async_computation.3 | async-start | bytes 5308416 | tf_op jit(solution)/shard_map/all_gather | solution.py:9
  9.2 101.7 %reduce-scatter.2.cloned.1.call-start = ((), (), s32[]{:S(2)}) async-start(), calls=%async_computation.1 | async-start | bytes 663552 | tf_op jit(solution)/shard_map/reduce_scatter | solution.py:38
  56.9 0.9 copy-start.1
  60.6 86.9 %all-reduce.2.cloned.1.call-start = ((), (), s32[]{:S(2)}) async-start(), calls=%async_computation.2 | async-start | bytes 147456 | tf_op jit(solution)/shard_map/psum | solution.py:39
Sparse Core Ops, SparseCore 0:
  9.4 41.4 all-gather.2
  60.7 50.1 reduce-scatter.1
  113.3 34.2 all-reduce.1
where the time goes:
time: 156 us
  waiting for transfers between devices  128 us (82%)
  between operations  13.1 us (8%)
  local copies, waits for them, and re-layouts  9.54 us (6%)
  matrix products  4.43 us (3%)
    reduce_scatter x1, waiting for transfers between devices, body(): lax.psum_scatter(conjugated, 'tm', scatter_dimension=0, tiled=True)  50.3 us
    all_gather x1, waiting for transfers between devices, carried_in(): gathered = lax.all_gather(part, axis)  41.5 us
    psum x1, waiting for transfers between devices, body(): return lax.psum(row_sums, 'group')  36.6 us
    while x1, local copies, waits for them, and re-layouts, carried_in(): return lax.fori_loop(0, place, one, state)  6.05 us
    dot_general x3, matrix products, times_high(): jnp.dot(left, right, precision=lax.Precision.HIGHEST, preferred_element_t...  4.43 us
    unnamed x5, local copies, waits for them, and re-layouts  3.49 us
  transfers between devices with their start and end apart: 3, of which 3 were waited for; matrix products, arithmetic and copies ran while one was open for 0% of the time, Pallas kernels for 0%

commit v1 on v0

--- a/solution.py
+++ b/solution.py
@@ -36,7 +36,7 @@
     pulled = times_high(perturbation[0], before)
     conjugated = times_high(prefix_rows.T, pulled)
     row_sums = lax.psum_scatter(conjugated, "tm", scatter_dimension=0, tiled=True)
-    return lax.psum(row_sums, "group")
+    return jnp.sum(lax.all_gather(row_sums, "group"), axis=0)
 
 
 def solution(mesh):

time: 156 us -> 133 us (0.85)
  waiting for transfers between devices: 128 us -> 91.8 us
  blocking collectives: 0 us -> 14.3 us
    psum x1 -> x0, waiting for transfers between devices: 36.6 us -> none  [body(): return lax.psum(row_sums, 'group')]
    all_gather x0 -> x1, blocking collectives: none -> 14.3 us  [body(): return jnp.sum(lax.all_gather(row_sums, 'group'), axis=0)]
    unnamed x5 -> x4, local copies, waits for them, and re-layouts: 3.49 us -> 1.97 us
  transfers between devices with their start and end apart: 3 -> 2, of which waited for: 3 -> 2; matrix products, arithmetic and copies ran while one was open for 0% -> 0% of each run, Pallas kernels for 0% -> 0%
where the time goes in v1:
time: 133 us
  waiting for transfers between devices  91.8 us (69%)
  blocking collectives  14.3 us (11%)
  between operations  13.4 us (10%)
  local copies, waits for them, and re-layouts  8.02 us (6%)
  matrix products  4.42 us (3%)
    reduce_scatter x1, waiting for transfers between devices, body(): lax.psum_scatter(conjugated, 'tm', scatter_dimension=0, tiled=True)  50.3 us
    all_gather x1, waiting for transfers between devices, carried_in(): gathered = lax.all_gather(part, axis)  41.5 us
    all_gather x1, blocking collectives, body(): return jnp.sum(lax.all_gather(row_sums, 'group'), axis=0)  14.3 us
    while x1, local copies, waits for them, and re-layouts, carried_in(): return lax.fori_loop(0, place, one, state)  6.05 us
    dot_general x3, matrix products, times_high(): jnp.dot(left, right, precision=lax.Precision.HIGHEST, preferred_element_t...  4.42 us
  transfers between devices with their start and end apart: 2, of which 2 were waited for; matrix products, arithmetic and copies ran while one was open for 0% of the time, Pallas kernels for 0%

profile of v1, /device:TPU:0, one launch (start us, length us, event | category | flops | bytes accessed | tf_op | source)
XLA Modules:
  0.0 132.8 jit_solution(10868188667320480218)
XLA Ops:
  6.5 0.0 copy-start
  6.5 0.0 all-gather.4.cloned.1.call-start
  6.5 1.1 copy-done
  7.6 1.6 %convolution_bitcast_fusion = f32[384,384]{0,1:T(8,128)} fusion(f32[1,384,384]{2,1,0:T(8,128)S(1)} %copy-done), kind=kOutput, calls=%fused_computation.4 | convolution fusion | flops 679772160 | bytes 1179648 | tf_op jit(solution)/shard_map/dot_general | solution.py:19
  9.2 0.0 all-gather.4.cloned.1.call-update
  9.2 0.0 reduce-scatter.2.cloned.1.call-start
  9.3 41.5 %all-gather.4.cloned.1.call-done = f32[3072,384]{0,1:T(8,128)} async-done(((f32[384,384]{0,1:T(8,128)}), f32[3072,384]{0,1:T(8,128)}) %all-gather.4.cloned.1.call-update) | async-done | bytes 4718608 | tf_op jit(solution)/shard_map/all_gather | solution.py:9
  50.8 6.0 %copy.4 = f32[3072,384]{1,0:T(8,128)} copy(f32[3072,384]{0,1:T(8,128)} %all-gather.4.cloned.1.call-done) | data formatting | bytes 9437184 | tf_op jit(solution)/shard_map/while | solution.py:15
  56.9 0.0 copy-start.1
  56.9 0.9 copy-done.1
  57.8 1.1 fusion.8
  58.9 1.7 %fusion.10 = f32[384,384]{1,0:T(8,128)} fusion(f32[384,96]{1,0:T(8,128)S(1)} %fusion.8, f32[384,384]{1,0:T(8,128)S(1)} %get-tuple-element.28, s32[]{:T(128)S(6)} %select_n.7), kind=kOutput, calls=%fused_computation.11 | convolution fusion | flops 169869312 | bytes 933892 | tf_op jit(solution)/shard_map/dot_general | solution.py:19
  60.6 0.0 reduce-scatter.2.cloned.1.call-update
  60.6 50.3 %reduce-scatter.2.cloned.1.call-done = f32[48,384]{1,0:T(8,128)} async-done(((f32[384,384]{1,0:T(8,128)}), f32[48,384]{1,0:T(8,128)}) %reduce-scatter.2.cloned.1.call-update) | async-done | bytes 73744 | tf_op jit(solution)/shard_map/reduce_scatter | solution.py:38
  111.0 14.3 %all-gather.1 = f32[192,384]{1,0:T(8,128)S(1)} all-gather(f32[48,384]{1,0:T(8,128)} %reduce-scatter.2.cloned.1.call-done), channel_id=3, replica_groups=mesh['tm'=8,'group'=4] {'group'}, dimensions={0}, use_global_device_ids=true | all-gather | bytes 368640 | tf_op jit(solution)/shard_map/all_gather | solution.py:39
  125.3 0.7 reduce_sum.9
  (2 shorter events, 0.0 us)
Async XLA Ops:
  6.5 1.1 copy-start
  6.5 44.3 %all-gather.4.cloned.1.call-start = ((), (), s32[]{:S(2)}) async-start(), calls=%async_computation.2 | async-start | bytes 5308416 | tf_op jit(solution)/shard_map/all_gather | solution.py:9
  9.2 101.7 %reduce-scatter.2.cloned.1.call-start = ((), (), s32[]{:S(2)}) async-start(), calls=%async_computation.1 | async-start | bytes 663552 | tf_op jit(solution)/shard_map/reduce_scatter | solution.py:38
  56.9 0.9 copy-start.1
Sparse Core Ops, SparseCore 0:
  9.4 41.4 all-gather.3
  60.7 50.1 reduce-scatter.1
